TPU v7x, 256 devices: a whole 4x4x8 slice. The times are simulated.
256 devices in a mesh: tm: 8 (over y, core), space: 32 (over x, z).
Axes of the slice: x: 4, y: 4, z: 8, core: 2. Of those that a mesh axis runs over, the one named last changes fastest.
Arguments:
- snapshots: float32 [2048, 128, 1024], P('space', None, 'tm'), may hold values from -6 to 6
- land_mask: int32 [2048, 128], P('space'), may hold values 0 or 1
- taps_rows: float32 [6], replicated, may hold values from -2.5 to 2.5
- taps_cols: float32 [6], replicated, may hold values from -2.5 to 2.5
- probes: float32 [1024, 64, 128], P('space'), may hold values from -6 to 6
Outputs:
- basis: float32 [1024, 64, 128], P('space', None, 'tm')
- coefficients: float32 [128, 128], P('tm')
All inputs are finite; a program needn't handle non-finite values. No bound on the sum of `land_mask` on one device may be relied on, other than what follows from the above.
Results may differ from a plain program's by a relative error of at most 0.00028.
Values sent between devices are 32-bit elements; how exact they have to be, the bound alone decides.
A program may use at most 64 MiB of HBM per device.

v0:
```python
import jax
import jax.numpy as jnp
from jax import lax
from jax.sharding import PartitionSpec as P

SIGN_STEPS = 8
exact_dot = lax.Precision.HIGHEST


def padded_2(x, sides, width):
    for axis, dim in sides:
        size, length = (lax.axis_size(axis), x.shape[dim])
        up = [(i, (i + 1) % size) for i in range(size - 1)]
        down = [(j, i) for i, j in up]
        last = lax.slice_in_dim(x, length - width, length, axis=dim)
        initial = lax.slice_in_dim(x, 0, width, axis=dim)
        before = lax.ppermute(last, axis, up)
        after = lax.ppermute(initial, axis, down)
        x = jnp.concatenate([before, x, after], axis=dim)
    return x


def partner(block, axis, distance):
    count = lax.axis_size(axis)
    route = []
    for low in range(count):
        high = low | 1 << distance
        if high != low and high < count:
            route += [(low, high), (high, low)]
    return lax.ppermute(block, axis, route)


def band_matrix(tap_values, out_count, in_width, shift_by):
    row_ids = lax.broadcasted_iota(jnp.int32, (out_count, in_width), 0)
    col_ids = lax.broadcasted_iota(jnp.int32, (out_count, in_width), 1)
    tap_offset = col_ids - 2 * row_ids - shift_by
    band_table = jnp.zeros((out_count, in_width), jnp.float32)
    for tap_index in range(6):
        band_table = band_table + jnp.where(tap_offset == tap_index, tap_values[tap_index], 0.0)
    return band_table


def merge_level(paired):
    partial_gram = jnp.einsum("gra,grb->gab", paired, paired, precision=exact_dot)
    gram_total = lax.psum(partial_gram, "space")
    order_size = gram_total.shape[-1]
    identity = jnp.eye(order_size, dtype=jnp.float32)
    mean_eig = jnp.sum(gram_total * identity, axis=(1, 2)) / order_size
    shifted = gram_total - mean_eig[:, None, None] * identity
    norm_scale = jnp.sqrt(jnp.sum(shifted * shifted, axis=(1, 2)) + 1e-06)
    sign_iter = shifted / norm_scale[:, None, None]
    for sweep_index in range(SIGN_STEPS):
        square = jnp.einsum("gab,gbc->gac", sign_iter, sign_iter, precision=exact_dot)
        sign_iter = 1.5 * sign_iter - 0.5 * jnp.einsum(
            "gab,gbc->gac", sign_iter, square, precision=exact_dot
        )
    projector = 0.5 * (identity + sign_iter)
    half_order = order_size // 2
    combine = projector[:, :, :half_order] + projector[:, :, half_order:]
    return jnp.einsum("gra,gab->grb", paired, combine, precision=exact_dot)


def local(snapshots, land_mask, taps_rows, taps_cols, probes):
    rows_dev, cell_cols, columns = snapshots.shape
    ocean_field = snapshots * land_mask.astype(jnp.float32)[:, :, None]
    across = band_matrix(taps_cols, cell_cols // 2, cell_cols, -2)
    narrowed = jnp.einsum("jy,xys->xjs", across, ocean_field, precision=exact_dot)
    padded = padded_2(narrowed, (("space", 0),), 3)
    row_filter = band_matrix(taps_rows, rows_dev // 2, rows_dev + 6, 1)
    filtered = jnp.einsum("ip,pjs->ijs", row_filter, padded, precision=exact_dot)
    cell_rows = rows_dev // 2 * (cell_cols // 2)
    factor = filtered.reshape(cell_rows, columns)
    flat_probes = probes.reshape(cell_rows, probes.shape[2])
    levels = lax.axis_size("tm").bit_length() - 1
    position = lax.axis_index("tm")
    merged = factor
    for level_index in range(levels):
        partner_fac = partner(merged, "tm", level_index)
        is_upper = position >> level_index & 1 == 1
        lower_part = jnp.where(is_upper, partner_fac, merged)
        upper_part = jnp.where(is_upper, merged, partner_fac)
        merged = merge_level(jnp.concatenate([lower_part, upper_part], axis=1)[None])[0]
    width_dev = columns // lax.axis_size("tm")
    col_start = position * width_dev
    partial_coef = jnp.einsum("rs,rp->sp", merged, flat_probes, precision=exact_dot)
    coefficients = lax.psum(partial_coef, "space")
    basis_own = lax.dynamic_slice_in_dim(merged, col_start, width_dev, 1)
    coef_own = lax.dynamic_slice_in_dim(coefficients, col_start, width_dev, 0)
    return (basis_own.reshape(rows_dev // 2, cell_cols // 2, width_dev), coef_own)


def solution(mesh):
    placed = (P("space", None, "tm"), P("space", None), P(), P(), P("space", None, None))
    return jax.shard_map(
        local,
        mesh=mesh,
        in_specs=placed,
        out_specs=(P("space", None, "tm"), P("tm", None)),
        check_vma=False,
    )
```

profile of v0, /device:TPU:2, one launch (start us, length us, event | category | flops | bytes accessed | tf_op | source)
XLA Modules:
  0.0 723.5 jit_solution(15306966266729676532)
XLA Ops:
  9.5 9.0 %fusion.11 = f32[64,64,128]{2,1,0:T(8,128)S(1)} fusion(f32[64,128,128]{2,1,0:T(8,128)} %param.5, f32[64,128]{1,0:T(8,128)S(1)} %convert_element_type.22, f32[]{:T(128)} %bitcast.12, f32[]{:T(128)} %bitcast.11, f32[]{:T(128)} %bitcast.10, f32[]{:T(128)} %bitcast.9, f32[]{:T(128)} %bitcast.8, f32[]{:T(128)} %bitcast.7, s32[64]{0:T(128)S(1)} %iota_multiply_fusion), kind=kOutput, calls=%fused_computation.15 | convolution fusion | flops 806510592 | bytes 6324504 | tf_op jit(solution)/shard_map/jy,xys->xjs/dot_general | solution.py:67
  18.6 3.8 collective-permute-start
  22.4 5.8 collective-permute-start.1
  30.8 6.5 fusion.2
  38.9 1.9 collective-permute-done.2
  40.7 1.7 broadcast_select_fusion.1
  42.4 4.2 fusion.14
  47.1 145.3 %all-reduce.5.cloned.1.call-done = f32[1,256,256]{2,1,0:T(8,128)} async-done(((f32[1,256,256]{2,1,0:T(8,128)}), f32[1,256,256]{2,1,0:T(8,128)}) %all-reduce.5.cloned.1.call-update) | async-done | bytes 262160 | tf_op jit(solution)/shard_map/psum | solution.py:45
  194.6 1.6 multiply_reduce_fusion.2
  205.3 3.3 fusion.9
  210.1 19.3 %collective-permute-done.3 = f32[2048,128]{0,1:T(8,128)} collective-permute-done((f32[2048,128]{0,1:T(8,128)}, f32[2048,128]{0,1:T(8,128)}, u32[]{:S(2)}, u32[]{:S(2)}) %collective-permute-start.3) | collective-permute-done | bytes 1048608 | tf_op jit(solution)/shard_map/ppermute | solution.py:30
  229.4 1.7 broadcast_select_fusion.3
  231.1 2.6 fusion.15
  233.9 141.9 %all-reduce.7.cloned.1.call-done = f32[1,256,256]{2,1,0:T(8,128)} async-done(((f32[1,256,256]{2,1,0:T(8,128)}), f32[1,256,256]{2,1,0:T(8,128)}) %all-reduce.7.cloned.1.call-update) | async-done | bytes 262160 | tf_op jit(solution)/shard_map/psum | solution.py:45
  378.0 1.6 multiply_reduce_fusion.1
  388.7 2.3 fusion.7
  391.0 3.0 collective-permute-start.4
  394.0 19.3 %collective-permute-done.4 = f32[2048,128]{0,1:T(8,128)} collective-permute-done((f32[2048,128]{0,1:T(8,128)}, f32[2048,128]{0,1:T(8,128)}, u32[]{:S(2)}, u32[]{:S(2)}) %collective-permute-start.4) | collective-permute-done | bytes 1048608 | tf_op jit(solution)/shard_map/ppermute | solution.py:30
  413.3 1.7 broadcast_select_fusion.5
  415.0 2.6 fusion.16
  417.9 141.8 %all-reduce.9.cloned.1.call-done = f32[1,256,256]{2,1,0:T(8,128)} async-done(((f32[1,256,256]{2,1,0:T(8,128)}), f32[1,256,256]{2,1,0:T(8,128)}) %all-reduce.9.cloned.1.call-update) | async-done | bytes 262160 | tf_op jit(solution)/shard_map/psum | solution.py:45
  562.0 1.6 multiply_reduce_fusion
  574.0 1.8 fusion.268
  576.8 138.7 %all-reduce.11.cloned.1.call-done = f32[128,128]{1,0:T(8,128)} async-done(((f32[128,128]{1,0:T(8,128)}), f32[128,128]{1,0:T(8,128)}) %all-reduce.11.cloned.1.call-update) | async-done | bytes 65552 | tf_op jit(solution)/shard_map/psum | solution.py:86
  (86 shorter events, 42.0 us)
Async XLA Ops:
  7.2 566.8 %copy-start = (f32[32,64,128]{2,1,0:T(8,128)S(1)}, f32[32,64,128]{2,1,0:T(8,128)}, u32[]{:S(2)}) copy-start(f32[32,64,128]{2,1,0:T(8,128)} %param.9) | copy-start | bytes 3145732
  7.2 185.2 %all-reduce.5.cloned.1.call-start = ((), (), s32[]{:S(2)}) async-start(), calls=%async_computation | async-start | bytes 524288 | tf_op jit(solution)/shard_map/psum | solution.py:45
  9.5 18.7 %copy-start.4 = (f32[6]{0:T(128)S(1)}, f32[6]{0:T(128)}, u32[]{:S(2)}) copy-start(f32[6]{0:T(128)} %param.7) | copy-start | bytes 76
  18.6 10.5 %collective-permute-start = (f32[3,64,128]{2,1,0:T(8,128)S(1)}, f32[3,64,128]{2,1,0:T(8,128)S(1)}, u32[]{:S(2)}, u32[]{:S(2)}) collective-permute-start(f32[3,64,128]{2,1,0:T(8,128)S(1)} %get-tuple-element.10), channel_id=1, source_target_pairs={{0,1},{1,2},{2,3},{3,4},{4,5},{5,6},{6,7},{7,8},{8,9},{9,10},{10,1... | collective-permute-start | bytes 294920 | tf_op jit(solution)/shard_map/ppermute | solution.py:17
  22.4 8.0 %collective-permute-start.1 = (f32[3,64,128]{2,1,0:T(8,128)S(1)}, f32[3,64,128]{2,1,0:T(8,128)S(1)}, u32[]{:S(2)}, u32[]{:S(2)}) collective-permute-start(f32[3,64,128]{2,1,0:T(8,128)S(1)} %get-tuple-element.11), channel_id=1, source_target_pairs={{1,0},{2,1},{3,2},{4,3},{5,4},{6,5},{7,6},{8,7},{9,8},{10,9},{11,1... | collective-permute-start | bytes 294920 | tf_op jit(solution)/shard_map/ppermute | solution.py:18
  37.8 1.0 copy-start.3
  37.9 2.9 collective-permute-start.2
  46.6 329.2 %all-reduce.7.cloned.1.call-start = ((), (), s32[]{:S(2)}) async-start(), calls=%async_computation.1 | async-start | bytes 524288 | tf_op jit(solution)/shard_map/psum | solution.py:45
  208.6 20.8 %collective-permute-start.3 = (f32[2048,128]{0,1:T(8,128)}, f32[2048,128]{0,1:T(8,128)}, u32[]{:S(2)}, u32[]{:S(2)}) collective-permute-start(f32[2048,128]{0,1:T(8,128)} %fusion.9), channel_id=1, source_target_pairs={{0,64},{64,0},{32,96},{96,32},{128,192},{192,128},{160,224},{224,1... | collective-permute-start | bytes 3145736 | tf_op jit(solution)/shard_map/ppermute | solution.py:30
  233.7 326.0 %all-reduce.9.cloned.1.call-start = ((), (), s32[]{:S(2)}) async-start(), calls=%async_computation.2 | async-start | bytes 524288 | tf_op jit(solution)/shard_map/psum | solution.py:45
  391.0 22.3 %collective-permute-start.4 = (f32[2048,128]{0,1:T(8,128)}, f32[2048,128]{0,1:T(8,128)}, u32[]{:S(2)}, u32[]{:S(2)}) collective-permute-start(f32[2048,128]{0,1:T(8,128)} %fusion.7), channel_id=1, source_target_pairs={{0,128},{128,0},{32,160},{160,32},{64,192},{192,64},{96,224},{224,... | collective-permute-start | bytes 3145736 | tf_op jit(solution)/shard_map/ppermute | solution.py:30
  415.0 150.7 %copy-start.1 = (f32[2048,128]{0,1:T(8,128)}, f32[2048,128]{0,1:T(8,128)S(1)}, u32[]{:S(2)}) copy-start(f32[2048,128]{0,1:T(8,128)S(1)} %get-tuple-element.5) | copy-start | bytes 3145732
  417.6 297.8 %all-reduce.11.cloned.1.call-start = ((), (), s32[]{:S(2)}) async-start(), calls=%async_computation.3 | async-start | bytes 131072 | tf_op jit(solution)/shard_map/psum | solution.py:86
  570.3 2.4 copy-start.2
Sparse Core Ops, SparseCore 0:
  46.7 145.6 all-reduce.4
  233.8 141.9 all-reduce.6
  417.7 141.9 all-reduce.8
  575.9 139.4 all-reduce.10
where the time goes:
time: 731 us; the launch traced here: 724 us
  waiting for transfers between devices  610 us (83%)
  matrix products  58.2 us (8%)
  between operations  18.6 us (3%)
  other arithmetic  15.7 us (2%)
  starting transfers between devices  15.3 us (2%)
    psum x3, waiting for transfers between devices, merge_level(): gram_total = lax.psum(partial_gram, 'space')  429 us
    psum x1, waiting for transfers between devices, local(): coefficients = lax.psum(partial_coef, 'space')  139 us
    ppermute x3, waiting for transfers between devices, partner(): return lax.ppermute(block, axis, route)  40.4 us
  transfers between devices with their start and end apart: 9, of which 9 were waited for; matrix products, arithmetic and copies ran while one was open for 0% of the time, Pallas kernels for 0%

commit v1 on v0

--- a/solution.py
+++ b/solution.py
@@ -42,7 +42,7 @@
 
 def merge_level(paired):
     partial_gram = jnp.einsum("gra,grb->gab", paired, paired, precision=exact_dot)
-    gram_total = lax.psum(partial_gram, "space")
+    gram_total = jnp.sum(lax.all_gather(partial_gram, "space"), axis=0)
     order_size = gram_total.shape[-1]
     identity = jnp.eye(order_size, dtype=jnp.float32)
     mean_eig = jnp.sum(gram_total * identity, axis=(1, 2)) / order_size

time: 731 us -> 597 us (0.82)
  waiting for transfers between devices: 610 us -> 475 us
    psum x3 -> x0, waiting for transfers between devices: 429 us -> none  [merge_level(): gram_total = lax.psum(partial_gram, 'space')]
    all_gather x0 -> x3, waiting for transfers between devices: none -> 287 us  [merge_level(): gram_total = jnp.sum(lax.all_gather(partial_gram, 'space'), axis=0)]
    reduce_sum x0 -> x3, other arithmetic: none -> 11.8 us  [merge_level(): gram_total = jnp.sum(lax.all_gather(partial_gram, 'space'), axis=0)]
    ppermute x3, waiting for transfers between devices: 40.4 us -> 47.7 us  [partner(): return lax.ppermute(block, axis, route)]
where the time goes in v1:
time: 597 us; the launch traced here: 590 us
  waiting for transfers between devices  475 us (80%)
  matrix products  52 us (9%)
  other arithmetic  21.5 us (4%)
  between operations  18.6 us (3%)
  starting transfers between devices  15.3 us (3%)
  local copies, waits for them, and re-layouts  7.12 us (1%)
    all_gather x3, waiting for transfers between devices, merge_level(): gram_total = jnp.sum(lax.all_gather(partial_gram, 'space'), axis=0)  287 us
    psum x1, waiting for transfers between devices, local(): coefficients = lax.psum(partial_coef, 'space')  139 us
    ppermute x3, waiting for transfers between devices, partner(): return lax.ppermute(block, axis, route)  47.7 us
  transfers between devices with their start and end apart: 9, of which 9 were waited for; matrix products, arithmetic and copies ran while one was open for 0% of the time, Pallas kernels for 0%

profile of v1, /device:TPU:2, one launch (start us, length us, event | category | flops | bytes accessed | tf_op | source)
XLA Modules:
  0.0 589.6 jit_solution(4095015698481230483)
XLA Ops:
  7.2 1.5 fusion.198
  9.5 9.0 %fusion.11 = f32[64,64,128]{2,1,0:T(8,128)S(1)} fusion(f32[64,128,128]{2,1,0:T(8,128)} %param.5, f32[64,128]{1,0:T(8,128)S(1)} %convert_element_type.45, f32[]{:T(128)} %bitcast.12, f32[]{:T(128)} %bitcast.11, f32[]{:T(128)} %bitcast.10, f32[]{:T(128)} %bitcast.9, f32[]{:T(128)} %bitcast.8, f32[]{:T(128)} %bitcast.7, s32[64]{0:T(128)S(1)} %iota_multiply_fusion), kind=kOutput, calls=%fused_computation.15 | convolution fusion | flops 806510592 | bytes 6324504 | tf_op jit(solution)/shard_map/jy,xys->xjs/dot_general | solution.py:67
  18.6 3.8 collective-permute-start
  22.4 5.8 collective-permute-start.1
  30.8 6.5 %fusion.2 = f32[32,64,128]{2,0,1:T(8,128)S(1)} fusion(f32[70,64,128]{2,1,0:T(8,128)S(1)} %pad_maximum_fusion, f32[]{:T(128)} %bitcast.5, f32[]{:T(128)} %bitcast.4, f32[]{:T(128)} %bitcast.3, f32[]{:T(128)} %bitcast.2, f32[]{:T(128)} %bitcast.1, f32[]{:T(128)} %bitcast, s32[32]{0:T(128)S(1)} %iota_multiply_fusion.1), kind=kOutput, calls=%fused_computation.2 | convolution fusion | flops 220243520 | bytes 3342488 | tf_op jit(solution)/shard_map/ip,pjs->ijs/dot_general | solution.py:70
  38.9 1.9 collective-permute-done.2
  40.7 1.7 broadcast_select_fusion.1
  42.4 4.2 fusion.10
  47.1 97.5 %all-gather.7.cloned.1.call-done = f32[8192,256]{1,0:T(8,128)} async-done(((f32[256,256]{1,0:T(8,128)}), f32[8192,256]{1,0:T(8,128)}) %all-gather.7.cloned.1.call-update) | async-done | bytes 8388624 | tf_op jit(solution)/shard_map/all_gather | solution.py:45
  144.6 3.9 reduce.9
  157.5 3.3 fusion.9
  162.3 23.0 %collective-permute-done.3 = f32[2048,128]{0,1:T(8,128)} collective-permute-done((f32[2048,128]{0,1:T(8,128)}, f32[2048,128]{0,1:T(8,128)}, u32[]{:S(2)}, u32[]{:S(2)}) %collective-permute-start.3) | collective-permute-done | bytes 1048608 | tf_op jit(solution)/shard_map/ppermute | solution.py:30
  185.3 1.7 broadcast_select_fusion.3
  187.0 2.6 fusion.8
  189.8 94.8 %all-gather.9.cloned.1.call-done = f32[8192,256]{1,0:T(8,128)} async-done(((f32[256,256]{1,0:T(8,128)}), f32[8192,256]{1,0:T(8,128)}) %all-gather.9.cloned.1.call-update) | async-done | bytes 8388624 | tf_op jit(solution)/shard_map/all_gather | solution.py:45
  284.6 3.9 reduce.10
  297.4 2.3 fusion.7
  299.8 3.0 collective-permute-start.4
  302.8 22.9 %collective-permute-done.4 = f32[2048,128]{0,1:T(8,128)S(1)} collective-permute-done((f32[2048,128]{0,1:T(8,128)}, f32[2048,128]{0,1:T(8,128)S(1)}, u32[]{:S(2)}, u32[]{:S(2)}) %collective-permute-start.4) | collective-permute-done | bytes 1048608 | tf_op jit(solution)/shard_map/ppermute | solution.py:30
  328.1 2.6 fusion.6
  331.0 94.8 %all-gather.11.cloned.1.call-done = f32[8192,256]{1,0:T(8,128)} async-done(((f32[256,256]{1,0:T(8,128)}), f32[8192,256]{1,0:T(8,128)}) %all-gather.11.cloned.1.call-update) | async-done | bytes 8388624 | tf_op jit(solution)/shard_map/all_gather | solution.py:45
  425.8 3.9 reduce.11
  440.0 1.8 fusion.220
  442.8 138.8 %all-reduce.2.cloned.1.call-done = f32[128,128]{1,0:T(8,128)} async-done(((f32[128,128]{1,0:T(8,128)}), f32[128,128]{1,0:T(8,128)}) %all-reduce.2.cloned.1.call-update) | async-done | bytes 65552 | tf_op jit(solution)/shard_map/psum | solution.py:86
  (89 shorter events, 35.8 us)
Async XLA Ops:
  7.2 432.8 %copy-start = (f32[32,64,128]{2,1,0:T(8,128)S(1)}, f32[32,64,128]{2,1,0:T(8,128)}, u32[]{:S(2)}) copy-start(f32[32,64,128]{2,1,0:T(8,128)} %param.9) | copy-start | bytes 3145732
  7.2 137.5 %all-gather.7.cloned.1.call-start = ((), (), s32[]{:S(2)}) async-start(), calls=%async_computation.1 | async-start | bytes 8650752 | tf_op jit(solution)/shard_map/all_gather | solution.py:45
  9.5 18.7 %copy-start.4 = (f32[6]{0:T(128)S(1)}, f32[6]{0:T(128)}, u32[]{:S(2)}) copy-start(f32[6]{0:T(128)} %param.7) | copy-start | bytes 76
  18.6 10.5 %collective-permute-start = (f32[3,64,128]{2,1,0:T(8,128)S(1)}, f32[3,64,128]{2,1,0:T(8,128)S(1)}, u32[]{:S(2)}, u32[]{:S(2)}) collective-permute-start(f32[3,64,128]{2,1,0:T(8,128)S(1)} %get-tuple-element.10), channel_id=1, source_target_pairs={{0,1},{1,2},{2,3},{3,4},{4,5},{5,6},{6,7},{7,8},{8,9},{9,10},{10,1... | collective-permute-start | bytes 294920 | tf_op jit(solution)/shard_map/ppermute | solution.py:17
  22.4 8.0 %collective-permute-start.1 = (f32[3,64,128]{2,1,0:T(8,128)S(1)}, f32[3,64,128]{2,1,0:T(8,128)S(1)}, u32[]{:S(2)}, u32[]{:S(2)}) collective-permute-start(f32[3,64,128]{2,1,0:T(8,128)S(1)} %get-tuple-element.11), channel_id=1, source_target_pairs={{1,0},{2,1},{3,2},{4,3},{5,4},{6,5},{7,6},{8,7},{9,8},{10,9},{11,1... | collective-permute-start | bytes 294920 | tf_op jit(solution)/shard_map/ppermute | solution.py:18
  37.8 1.0 copy-start.3
  37.9 2.9 collective-permute-start.2
  46.6 238.0 %all-gather.9.cloned.1.call-start = ((), (), s32[]{:S(2)}) async-start(), calls=%async_computation.2 | async-start | bytes 8650752 | tf_op jit(solution)/shard_map/all_gather | solution.py:45
  160.8 24.5 %collective-permute-start.3 = (f32[2048,128]{0,1:T(8,128)}, f32[2048,128]{0,1:T(8,128)}, u32[]{:S(2)}, u32[]{:S(2)}) collective-permute-start(f32[2048,128]{0,1:T(8,128)} %fusion.9), channel_id=1, source_target_pairs={{0,64},{64,0},{32,96},{96,32},{128,192},{192,128},{160,224},{224,1... | collective-permute-start | bytes 3145736 | tf_op jit(solution)/shard_map/ppermute | solution.py:30
  189.6 236.2 %all-gather.11.cloned.1.call-start = ((), (), s32[]{:S(2)}) async-start(), calls=%async_computation.3 | async-start | bytes 8650752 | tf_op jit(solution)/shard_map/all_gather | solution.py:45
  299.8 25.9 %collective-permute-start.4 = (f32[2048,128]{0,1:T(8,128)}, f32[2048,128]{0,1:T(8,128)S(1)}, u32[]{:S(2)}, u32[]{:S(2)}) collective-permute-start(f32[2048,128]{0,1:T(8,128)} %fusion.7), channel_id=1, source_target_pairs={{0,128},{128,0},{32,160},{160,32},{64,192},{192,64},{96,224},{224,... | collective-permute-start | bytes 3145736 | tf_op jit(solution)/shard_map/ppermute | solution.py:30
  327.0 1.1 copy-start.1
  330.7 250.9 %all-reduce.2.cloned.1.call-start = ((), (), s32[]{:S(2)}) async-start(), calls=%async_computation | async-start | bytes 131072 | tf_op jit(solution)/shard_map/psum | solution.py:86
  436.7 2.0 copy-start.2
Sparse Core Ops, SparseCore 0:
  46.7 97.8 all-gather.6
  189.7 94.8 all-gather.8
  330.8 94.8 all-gather.10
  441.9 139.6 all-reduce.1
